TPU v7x, 32 devices: a whole 2x2x4 slice. The times are simulated.
32 devices in a mesh: groups: 2 (over x), row: 16 (over z, y, core).
Axes of the slice: x: 2, y: 2, z: 4, core: 2. Of those that a mesh axis runs over, the one named last changes fastest.
Arguments:
- orbitals: bfloat16 [4096, 512], P(('groups', 'row')), parts along dimension 0, may hold values from -1.296875 to 1.296875
- basis: bfloat16 [4096, 1024], P(('groups', 'row')), parts along dimension 0, may hold values from -0.1875 to 0.1875
- kernel: bfloat16 [4096, 2048], P(('groups', 'row')), parts along dimension 0, may hold values from -6 to 6
Outputs:
- exchange_matrix: float32 [2048, 1024], P('groups', 'row'), parts along dimension 0
There are 2 independent parts, one for each index of `groups`. A program takes and returns all parts, laid end to end along the dimension named above; each array names one. Nothing has to cross between parts.
All inputs are finite; a program needn't handle non-finite values.
Results may differ from a plain program's by a relative error of at most 0.0041.
Values may be sent and summed in bfloat16 or wider, within the bound.
A program may use at most 128 MiB of HBM per device.

v0:
```python
import jax
import jax.numpy as jnp
from jax import lax
from jax.sharding import PartitionSpec as P


def shards(orbitals, basis, kernel):
    density = lax.dot_general(
        orbitals,
        lax.all_gather(orbitals, "row", axis=0, tiled=True),
        (((1,), (1,)), ((), ())),
        preferred_element_type=jnp.float32,
    )
    weighted = (density * kernel.astype(jnp.float32)).astype(jnp.bfloat16)
    whole_basis = lax.all_gather(basis, "row", axis=0, tiled=True)
    applied = jnp.dot(weighted, whole_basis, preferred_element_type=jnp.float32).astype(
        jnp.bfloat16
    )
    received = lax.all_to_all(applied, "row", split_axis=1, concat_axis=0, tiled=True)
    exchange_matrix = lax.dot_general(
        whole_basis, received, (((0,), (0,)), ((), ())), preferred_element_type=jnp.float32
    )
    return exchange_matrix


def solution(mesh):
    return jax.shard_map(
        shards,
        mesh=mesh,
        in_specs=(
            P(("groups", "row"), None),
            P(("groups", "row"), None),
            P(("groups", "row"), None),
        ),
        out_specs=P("groups", "row"),
        check_vma=False,
    )
```

profile of v0, /device:TPU:0, one launch (start us, length us, event | category | flops | bytes accessed | tf_op | source)
XLA Modules:
  0.0 133.2 jit_solution(10812226006285130068)
XLA Ops:
  6.5 0.0 all-gather.3.cloned.1.call-start
  6.5 0.7 all-gather.3.cloned.1.call-update
  7.3 0.0 all-gather.5.cloned.1.call-start
  7.3 0.7 all-gather.5.cloned.1.call-update
  8.0 45.7 %all-gather.3.cloned.1.call-done = bf16[2048,512]{1,0:T(8,128)(2,1)} async-done(((bf16[128,512]{1,0:T(8,128)(2,1)}), bf16[2048,512]{1,0:T(8,128)(2,1)}) %all-gather.3.cloned.1.call-update) | async-done | bytes 2097168 | tf_op jit(solution)/shard_map/all_gather | solution.py:10
  53.7 51.3 %all-gather.5.cloned.1.call-done = bf16[2048,1024]{1,0:T(8,128)(2,1)} async-done(((bf16[128,1024]{1,0:T(8,128)(2,1)}), bf16[2048,1024]{1,0:T(8,128)(2,1)}) %all-gather.5.cloned.1.call-update) | async-done | bytes 4194320 | tf_op jit(solution)/shard_map/all_gather | solution.py:15
  105.0 4.4 %convolution_convert_fusion = bf16[128,1024]{1,0:T(8,128)(2,1)S(1)} fusion(bf16[2048,1024]{1,0:T(8,128)(2,1)} %all-gather.5.cloned.1.call-done, bf16[128,512]{1,0:T(8,128)(2,1)} %param.3, bf16[2048,512]{1,0:T(8,128)(2,1)} %all-gather.3.cloned.1.call-done, bf16[128,2048]{1,0:T(8,128)(2,1)} %param.5), kind=kOutput, calls=%fused_computation.2 | convolution fusion | flops 806223872 | bytes 7208960 | tf_op jit(solution)/shard_map/dot_general | solution.py:16
  109.4 0.2 copy.4
  109.6 13.1 %all_to_all.19 = bf16[128,16,64]{0,2,1:T(8,128)(2,1)S(1)} all-to-all(bf16[128,16,64]{0,2,1:T(8,128)(2,1)S(1)} %bitcast.15), channel_id=1, replica_groups=mesh['groups'=2,'row'=16] {'row'}, dimensions={1} | all-to-all | bytes 524288 | tf_op jit(solution)/shard_map/all_to_all | solution.py:19
  122.6 3.7 %convolution_bitcast_fusion = f32[1024,64]{0,1:T(8,128)} fusion(bf16[2048,1024]{1,0:T(8,128)(2,1)} %all-gather.5.cloned.1.call-done, bf16[128,16,64]{0,2,1:T(8,128)(2,1)S(1)} %all_to_all.19), kind=kOutput, calls=%fused_computation.3 | convolution fusion | flops 268435456 | bytes 4718592 | tf_op jit(solution)/shard_map/dot_general | solution.py:20
Async XLA Ops:
  6.5 47.2 %all-gather.3.cloned.1.call-start = ((), (), s32[]{:S(2)}) async-start(), calls=%async_computation.1 | async-start | bytes 2228224 | tf_op jit(solution)/shard_map/all_gather | solution.py:10
  7.3 97.7 %all-gather.5.cloned.1.call-start = ((), (), s32[]{:S(2)}) async-start(), calls=%async_computation.2 | async-start | bytes 4456448 | tf_op jit(solution)/shard_map/all_gather | solution.py:15
Sparse Core Ops, SparseCore 0:
  9.5 44.1 all-gather.2
  55.9 49.0 all-gather.4
where the time goes:
time: 133 us
  waiting for transfers between devices  98.4 us (74%)
  between operations  13.4 us (10%)
  blocking collectives  13.1 us (10%)
  matrix products  8.13 us (6%)
    all_gather x1, waiting for transfers between devices, shards(): whole_basis = lax.all_gather(basis, 'row', axis=0, tiled=True)  51.3 us
    all_gather x1, waiting for transfers between devices, shards(): lax.all_gather(orbitals, 'row', axis=0, tiled=True)  45.7 us
    all_to_all x1, blocking collectives, shards(): lax.all_to_all(applied, 'row', split_axis=1, concat_axis=0, tiled=True)  13.1 us
    dot_general x1, matrix products, shards(): jnp.dot(weighted, whole_basis, preferred_element_type=jnp.float32)  4.39 us
    dot_general x1, matrix products, shards(): lax.dot_general(whole_basis, received, (((0,), (0,)), ((), ())), preferre...  3.73 us
  transfers between devices with their start and end apart: 2, of which 2 were waited for; matrix products, arithmetic and copies ran while one was open for 0% of the time, Pallas kernels for 0%

commit v1 on v0

--- a/solution.py
+++ b/solution.py
@@ -16,7 +16,19 @@
     applied = jnp.dot(weighted, whole_basis, preferred_element_type=jnp.float32).astype(
         jnp.bfloat16
     )
-    received = lax.all_to_all(applied, "row", split_axis=1, concat_axis=0, tiled=True)
+    ways, here = (lax.axis_size("row"), lax.axis_index("row"))
+    width = applied.shape[1] // ways
+    dims = list(applied.shape)
+    dims[1] = width
+    height = dims[0]
+    dims[0] = height * ways
+    full = jnp.zeros(dims, applied.dtype)
+    for mask in range(ways):
+        part = lax.dynamic_slice_in_dim(applied, (here ^ mask) * width, width, axis=1)
+        if mask:
+            part = lax.ppermute(part, "row", [(d, d ^ mask) for d in range(ways)])
+        full = lax.dynamic_update_slice_in_dim(full, part, (here ^ mask) * height, axis=0)
+    received = full
     exchange_matrix = lax.dot_general(
         whole_basis, received, (((0,), (0,)), ((), ())), preferred_element_type=jnp.float32
     )

time: 133 us -> 146 us (1.098)
  starting transfers between devices: 0.04 us -> 21.1 us
  blocking collectives: 13.1 us -> 0 us
  waiting for transfers between devices: 98.4 us -> 102 us
    ppermute x0 -> x15, starting transfers between devices: none -> 21.1 us  [shards(): part = lax.ppermute(part, 'row', [(d, d ^ mask) for d in range(ways)])]
    all_to_all x1 -> x0, blocking collectives: 13.1 us -> none  [shards(): lax.all_to_all(applied, 'row', split_axis=1, concat_axis=0, tiled=True)]
    ppermute x0 -> x15, waiting for transfers between devices: none -> 3.9 us  [shards(): part = lax.ppermute(part, 'row', [(d, d ^ mask) for d in range(ways)])]
  transfers between devices with their start and end apart: 2 -> 17, of which waited for: 2 -> 4; matrix products, arithmetic and copies ran while one was open for 0% -> 0% of each run, Pallas kernels for 0% -> 0%
where the time goes in v1:
time: 146 us
  waiting for transfers between devices  102 us (70%)
  starting transfers between devices  21.1 us (14%)
  between operations  13.6 us (9%)
  matrix products  8.15 us (6%)
    all_gather x1, waiting for transfers between devices, shards(): whole_basis = lax.all_gather(basis, 'row', axis=0, tiled=True)  51.3 us
    all_gather x1, waiting for transfers between devices, shards(): lax.all_gather(orbitals, 'row', axis=0, tiled=True)  45.6 us
    ppermute x15, starting transfers between devices, shards(): part = lax.ppermute(part, 'row', [(d, d ^ mask) for d in range(ways)])  21.1 us
    dot_general x1, matrix products, shards(): jnp.dot(weighted, whole_basis, preferred_element_type=jnp.float32)  4.39 us
    ppermute x15, waiting for transfers between devices, shards(): part = lax.ppermute(part, 'row', [(d, d ^ mask) for d in range(ways)])  3.9 us
    dot_general x1, matrix products, shards(): lax.dot_general(whole_basis, received, (((0,), (0,)), ((), ())), preferre...  3.76 us
  transfers between devices with their start and end apart: 17, of which 4 were waited for; matrix products, arithmetic and copies ran while one was open for 0% of the time, Pallas kernels for 0%

profile of v1, /device:TPU:0, one launch (start us, length us, event | category | flops | bytes accessed | tf_op | source)
XLA Modules:
  0.0 145.6 jit_solution(16061802133155719486)
XLA Ops:
  6.5 0.0 all-gather.3.cloned.1.call-start
  6.5 0.7 all-gather.3.cloned.1.call-update
  7.3 0.0 all-gather.5.cloned.1.call-start
  7.3 0.7 all-gather.5.cloned.1.call-update
  8.1 45.6 %all-gather.3.cloned.1.call-done = bf16[2048,512]{1,0:T(8,128)(2,1)} async-done(((bf16[128,512]{1,0:T(8,128)(2,1)}), bf16[2048,512]{1,0:T(8,128)(2,1)}) %all-gather.3.cloned.1.call-update) | async-done | bytes 2097168 | tf_op jit(solution)/shard_map/all_gather | solution.py:10
  53.7 51.3 %all-gather.5.cloned.1.call-done = bf16[2048,1024]{1,0:T(8,128)(2,1)} async-done(((bf16[128,1024]{1,0:T(8,128)(2,1)}), bf16[2048,1024]{1,0:T(8,128)(2,1)}) %all-gather.5.cloned.1.call-update) | async-done | bytes 4194320 | tf_op jit(solution)/shard_map/all_gather | solution.py:15
  105.0 4.4 %convolution_convert_fusion = bf16[128,1024]{1,0:T(8,128)(2,1)S(1)} fusion(bf16[2048,1024]{1,0:T(8,128)(2,1)} %all-gather.5.cloned.1.call-done, bf16[128,512]{1,0:T(8,128)(2,1)} %param.3, bf16[2048,512]{1,0:T(8,128)(2,1)} %all-gather.3.cloned.1.call-done, bf16[128,2048]{1,0:T(8,128)(2,1)} %param.5), kind=kOutput, calls=%fused_computation.2 | convolution fusion | flops 806223872 | bytes 7208960 | tf_op jit(solution)/shard_map/dot_general | solution.py:16
  109.4 0.1 broadcast_in_dim.3
  109.5 0.3 constant_dynamic-slice_fusion
  109.8 0.3 collective-permute-start
  110.1 0.6 collective-permute-start.1
  110.7 1.1 collective-permute-start.2
  111.8 1.5 %collective-permute-start.3 = (bf16[128,64]{1,0:T(8,128)(2,1)S(1)}, bf16[128,64]{1,0:T(8,128)(2,1)S(1)}, u32[]{:S(2)}, u32[]{:S(2)}) collective-permute-start(bf16[128,64]{1,0:T(8,128)(2,1)S(1)} %get-tuple-element.16), channel_id=1, source_target_pairs={{0,4},{1,5},{2,6},{3,7},{4,0},{5,1},{6,2},{7,3},{8,12},{9,13},{10,... | collective-permute-start | bytes 49160 | tf_op jit(solution)/shard_map/ppermute | solution.py:29
  113.3 0.3 collective-permute-start.4
  113.6 0.0 collective-permute-done
  113.6 1.5 %collective-permute-start.5 = (bf16[128,64]{1,0:T(8,128)(2,1)S(1)}, bf16[128,64]{1,0:T(8,128)(2,1)S(1)}, u32[]{:S(2)}, u32[]{:S(2)}) collective-permute-start(bf16[128,64]{1,0:T(8,128)(2,1)S(1)} %get-tuple-element.14), channel_id=1, source_target_pairs={{0,6},{1,7},{2,4},{3,5},{4,2},{5,3},{6,0},{7,1},{8,14},{9,15},{10,... | collective-permute-start | bytes 49160 | tf_op jit(solution)/shard_map/ppermute | solution.py:29
  115.2 0.0 collective-permute-done.1
  115.2 1.0 collective-permute-start.6
  116.2 0.0 collective-permute-done.2
  116.2 1.9 %collective-permute-start.7 = (bf16[128,64]{1,0:T(8,128)(2,1)S(1)}, bf16[128,64]{1,0:T(8,128)(2,1)S(1)}, u32[]{:S(2)}, u32[]{:S(2)}) collective-permute-start(bf16[128,64]{1,0:T(8,128)(2,1)S(1)} %get-tuple-element.12), channel_id=1, source_target_pairs={{0,8},{1,9},{2,10},{3,11},{4,12},{5,13},{6,14},{7,15},{8,0},{9,1},... | collective-permute-start | bytes 49160 | tf_op jit(solution)/shard_map/ppermute | solution.py:29
  118.2 0.0 collective-permute-done.3
  118.2 1.0 collective-permute-start.8
  119.2 0.0 collective-permute-done.4
  119.2 1.9 %collective-permute-start.9 = (bf16[128,64]{1,0:T(8,128)(2,1)S(1)}, bf16[128,64]{1,0:T(8,128)(2,1)S(1)}, u32[]{:S(2)}, u32[]{:S(2)}) collective-permute-start(bf16[128,64]{1,0:T(8,128)(2,1)S(1)} %get-tuple-element.10), channel_id=1, source_target_pairs={{0,10},{1,11},{2,8},{3,9},{4,14},{5,15},{6,12},{7,13},{8,2},{9,3},... | collective-permute-start | bytes 49160 | tf_op jit(solution)/shard_map/ppermute | solution.py:29
  121.1 0.0 collective-permute-done.5
  121.1 1.6 %collective-permute-start.10 = (bf16[128,64]{1,0:T(8,128)(2,1)S(1)}, bf16[128,64]{1,0:T(8,128)(2,1)S(1)}, u32[]{:S(2)}, u32[]{:S(2)}) collective-permute-start(bf16[128,64]{1,0:T(8,128)(2,1)S(1)} %get-tuple-element.9), channel_id=1, source_target_pairs={{0,11},{1,10},{2,9},{3,8},{4,15},{5,14},{6,13},{7,12},{8,3},{9,2},... | collective-permute-start | bytes 49160 | tf_op jit(solution)/shard_map/ppermute | solution.py:29
  122.7 0.0 collective-permute-done.6
  122.7 1.9 %collective-permute-start.11 = (bf16[128,64]{1,0:T(8,128)(2,1)S(1)}, bf16[128,64]{1,0:T(8,128)(2,1)S(1)}, u32[]{:S(2)}, u32[]{:S(2)}) collective-permute-start(bf16[128,64]{1,0:T(8,128)(2,1)S(1)} %get-tuple-element.8), channel_id=1, source_target_pairs={{0,12},{1,13},{2,14},{3,15},{4,8},{5,9},{6,10},{7,11},{8,4},{9,5},... | collective-permute-start | bytes 49160 | tf_op jit(solution)/shard_map/ppermute | solution.py:29
  124.7 0.0 collective-permute-done.7
  124.7 1.9 %collective-permute-start.12 = (bf16[128,64]{1,0:T(8,128)(2,1)S(1)}, bf16[128,64]{1,0:T(8,128)(2,1)S(1)}, u32[]{:S(2)}, u32[]{:S(2)}) collective-permute-start(bf16[128,64]{1,0:T(8,128)(2,1)S(1)} %get-tuple-element.7), channel_id=1, source_target_pairs={{0,13},{1,12},{2,15},{3,14},{4,9},{5,8},{6,11},{7,10},{8,5},{9,4},... | collective-permute-start | bytes 49160 | tf_op jit(solution)/shard_map/ppermute | solution.py:29
  126.6 0.0 collective-permute-done.8
  126.6 2.0 %collective-permute-start.13 = (bf16[128,64]{1,0:T(8,128)(2,1)S(1)}, bf16[128,64]{1,0:T(8,128)(2,1)S(1)}, u32[]{:S(2)}, u32[]{:S(2)}) collective-permute-start(bf16[128,64]{1,0:T(8,128)(2,1)S(1)} %get-tuple-element.6), channel_id=1, source_target_pairs={{0,14},{1,15},{2,12},{3,13},{4,10},{5,11},{6,8},{7,9},{8,6},{9,7},... | collective-permute-start | bytes 49160 | tf_op jit(solution)/shard_map/ppermute | solution.py:29
  128.6 0.0 collective-permute-done.9
  128.6 2.4 %collective-permute-start.14 = (bf16[128,64]{1,0:T(8,128)(2,1)S(1)}, bf16[128,64]{1,0:T(8,128)(2,1)S(1)}, u32[]{:S(2)}, u32[]{:S(2)}) collective-permute-start(bf16[128,64]{1,0:T(8,128)(2,1)S(1)} %get-tuple-element.5), channel_id=1, source_target_pairs={{0,15},{1,14},{2,13},{3,12},{4,11},{5,10},{6,9},{7,8},{8,7},{9,6},... | collective-permute-start | bytes 49160 | tf_op jit(solution)/shard_map/ppermute | solution.py:29
  131.0 0.0 collective-permute-done.10
  131.1 0.0 collective-permute-done.11
  131.1 0.0 collective-permute-done.12
  131.1 2.1 %collective-permute-done.13 = bf16[128,64]{1,0:T(8,128)(2,1)S(1)} collective-permute-done((bf16[128,64]{1,0:T(8,128)(2,1)S(1)}, bf16[128,64]{1,0:T(8,128)(2,1)S(1)}, u32[]{:S(2)}, u32[]{:S(2)}) %collective-permute-start.13) | collective-permute-done | bytes 16416 | tf_op jit(solution)/shard_map/ppermute | solution.py:29
  133.3 1.7 %collective-permute-done.14 = bf16[128,64]{1,0:T(8,128)(2,1)S(1)} collective-permute-done((bf16[128,64]{1,0:T(8,128)(2,1)S(1)}, bf16[128,64]{1,0:T(8,128)(2,1)S(1)}, u32[]{:S(2)}, u32[]{:S(2)}) %collective-permute-start.14) | collective-permute-done | bytes 16416 | tf_op jit(solution)/shard_map/ppermute | solution.py:29
  135.0 3.8 %convolution_bitcast_fusion = f32[1024,64]{0,1:T(8,128)} fusion(bf16[2048,64]{1,0:T(8,128)(2,1)S(1)} %constant_dynamic-update-slice_fusion.14, bf16[2048,1024]{1,0:T(8,128)(2,1)} %all-gather.5.cloned.1.call-done), kind=kOutput, calls=%fused_computation.3 | convolution fusion | flops 268435456 | bytes 4718592 | tf_op jit(solution)/shard_map/dot_general | solution.py:32
  (15 shorter events, 0.2 us)
Async XLA Ops:
  6.5 47.2 %all-gather.3.cloned.1.call-start = ((), (), s32[]{:S(2)}) async-start(), calls=%async_computation | async-start | bytes 2228224 | tf_op jit(solution)/shard_map/all_gather | solution.py:10
  7.3 97.7 %all-gather.5.cloned.1.call-start = ((), (), s32[]{:S(2)}) async-start(), calls=%async_computation.1 | async-start | bytes 4456448 | tf_op jit(solution)/shard_map/all_gather | solution.py:15
  109.8 3.8 %collective-permute-start = (bf16[128,64]{1,0:T(8,128)(2,1)S(1)}, bf16[128,64]{1,0:T(8,128)(2,1)S(1)}, u32[]{:S(2)}, u32[]{:S(2)}) collective-permute-start(bf16[128,64]{1,0:T(8,128)(2,1)S(1)} %get-tuple-element.19), channel_id=1, source_target_pairs={{0,1},{1,0},{2,3},{3,2},{4,5},{5,4},{6,7},{7,6},{8,9},{9,8},{10,11... | collective-permute-start | bytes 49160 | tf_op jit(solution)/shard_map/ppermute | solution.py:29
  110.1 5.0 %collective-permute-start.1 = (bf16[128,64]{1,0:T(8,128)(2,1)S(1)}, bf16[128,64]{1,0:T(8,128)(2,1)S(1)}, u32[]{:S(2)}, u32[]{:S(2)}) collective-permute-start(bf16[128,64]{1,0:T(8,128)(2,1)S(1)} %get-tuple-element.18), channel_id=1, source_target_pairs={{0,2},{1,3},{2,0},{3,1},{4,6},{5,7},{6,4},{7,5},{8,10},{9,11},{10,... | collective-permute-start | bytes 49160 | tf_op jit(solution)/shard_map/ppermute | solution.py:29
  110.7 5.5 %collective-permute-start.2 = (bf16[128,64]{1,0:T(8,128)(2,1)S(1)}, bf16[128,64]{1,0:T(8,128)(2,1)S(1)}, u32[]{:S(2)}, u32[]{:S(2)}) collective-permute-start(bf16[128,64]{1,0:T(8,128)(2,1)S(1)} %get-tuple-element.17), channel_id=1, source_target_pairs={{0,3},{1,2},{2,1},{3,0},{4,7},{5,6},{6,5},{7,4},{8,11},{9,10},{10,... | collective-permute-start | bytes 49160 | tf_op jit(solution)/shard_map/ppermute | solution.py:29
  111.8 6.4 %collective-permute-start.3 = (bf16[128,64]{1,0:T(8,128)(2,1)S(1)}, bf16[128,64]{1,0:T(8,128)(2,1)S(1)}, u32[]{:S(2)}, u32[]{:S(2)}) collective-permute-start(bf16[128,64]{1,0:T(8,128)(2,1)S(1)} %get-tuple-element.16), channel_id=1, source_target_pairs={{0,4},{1,5},{2,6},{3,7},{4,0},{5,1},{6,2},{7,3},{8,12},{9,13},{10,... | collective-permute-start | bytes 49160 | tf_op jit(solution)/shard_map/ppermute | solution.py:29
  113.3 5.9 %collective-permute-start.4 = (bf16[128,64]{1,0:T(8,128)(2,1)S(1)}, bf16[128,64]{1,0:T(8,128)(2,1)S(1)}, u32[]{:S(2)}, u32[]{:S(2)}) collective-permute-start(bf16[128,64]{1,0:T(8,128)(2,1)S(1)} %get-tuple-element.15), channel_id=1, source_target_pairs={{0,5},{1,4},{2,7},{3,6},{4,1},{5,0},{6,3},{7,2},{8,13},{9,12},{10,... | collective-permute-start | bytes 49160 | tf_op jit(solution)/shard_map/ppermute | solution.py:29
  113.6 7.5 %collective-permute-start.5 = (bf16[128,64]{1,0:T(8,128)(2,1)S(1)}, bf16[128,64]{1,0:T(8,128)(2,1)S(1)}, u32[]{:S(2)}, u32[]{:S(2)}) collective-permute-start(bf16[128,64]{1,0:T(8,128)(2,1)S(1)} %get-tuple-element.14), channel_id=1, source_target_pairs={{0,6},{1,7},{2,4},{3,5},{4,2},{5,3},{6,0},{7,1},{8,14},{9,15},{10,... | collective-permute-start | bytes 49160 | tf_op jit(solution)/shard_map/ppermute | solution.py:29
  115.2 7.6 %collective-permute-start.6 = (bf16[128,64]{1,0:T(8,128)(2,1)S(1)}, bf16[128,64]{1,0:T(8,128)(2,1)S(1)}, u32[]{:S(2)}, u32[]{:S(2)}) collective-permute-start(bf16[128,64]{1,0:T(8,128)(2,1)S(1)} %get-tuple-element.13), channel_id=1, source_target_pairs={{0,7},{1,6},{2,5},{3,4},{4,3},{5,2},{6,1},{7,0},{8,15},{9,14},{10,... | collective-permute-start | bytes 49160 | tf_op jit(solution)/shard_map/ppermute | solution.py:29
  116.2 8.4 %collective-permute-start.7 = (bf16[128,64]{1,0:T(8,128)(2,1)S(1)}, bf16[128,64]{1,0:T(8,128)(2,1)S(1)}, u32[]{:S(2)}, u32[]{:S(2)}) collective-permute-start(bf16[128,64]{1,0:T(8,128)(2,1)S(1)} %get-tuple-element.12), channel_id=1, source_target_pairs={{0,8},{1,9},{2,10},{3,11},{4,12},{5,13},{6,14},{7,15},{8,0},{9,1},... | collective-permute-start | bytes 49160 | tf_op jit(solution)/shard_map/ppermute | solution.py:29
  118.2 8.4 %collective-permute-start.8 = (bf16[128,64]{1,0:T(8,128)(2,1)S(1)}, bf16[128,64]{1,0:T(8,128)(2,1)S(1)}, u32[]{:S(2)}, u32[]{:S(2)}) collective-permute-start(bf16[128,64]{1,0:T(8,128)(2,1)S(1)} %get-tuple-element.11), channel_id=1, source_target_pairs={{0,9},{1,8},{2,11},{3,10},{4,13},{5,12},{6,15},{7,14},{8,1},{9,0},... | collective-permute-start | bytes 49160 | tf_op jit(solution)/shard_map/ppermute | solution.py:29
  119.2 9.4 %collective-permute-start.9 = (bf16[128,64]{1,0:T(8,128)(2,1)S(1)}, bf16[128,64]{1,0:T(8,128)(2,1)S(1)}, u32[]{:S(2)}, u32[]{:S(2)}) collective-permute-start(bf16[128,64]{1,0:T(8,128)(2,1)S(1)} %get-tuple-element.10), channel_id=1, source_target_pairs={{0,10},{1,11},{2,8},{3,9},{4,14},{5,15},{6,12},{7,13},{8,2},{9,3},... | collective-permute-start | bytes 49160 | tf_op jit(solution)/shard_map/ppermute | solution.py:29
  121.1 9.9 %collective-permute-start.10 = (bf16[128,64]{1,0:T(8,128)(2,1)S(1)}, bf16[128,64]{1,0:T(8,128)(2,1)S(1)}, u32[]{:S(2)}, u32[]{:S(2)}) collective-permute-start(bf16[128,64]{1,0:T(8,128)(2,1)S(1)} %get-tuple-element.9), channel_id=1, source_target_pairs={{0,11},{1,10},{2,9},{3,8},{4,15},{5,14},{6,13},{7,12},{8,3},{9,2},... | collective-permute-start | bytes 49160 | tf_op jit(solution)/shard_map/ppermute | solution.py:29
  122.7 8.3 %collective-permute-start.11 = (bf16[128,64]{1,0:T(8,128)(2,1)S(1)}, bf16[128,64]{1,0:T(8,128)(2,1)S(1)}, u32[]{:S(2)}, u32[]{:S(2)}) collective-permute-start(bf16[128,64]{1,0:T(8,128)(2,1)S(1)} %get-tuple-element.8), channel_id=1, source_target_pairs={{0,12},{1,13},{2,14},{3,15},{4,8},{5,9},{6,10},{7,11},{8,4},{9,5},... | collective-permute-start | bytes 49160 | tf_op jit(solution)/shard_map/ppermute | solution.py:29
  124.7 6.4 %collective-permute-start.12 = (bf16[128,64]{1,0:T(8,128)(2,1)S(1)}, bf16[128,64]{1,0:T(8,128)(2,1)S(1)}, u32[]{:S(2)}, u32[]{:S(2)}) collective-permute-start(bf16[128,64]{1,0:T(8,128)(2,1)S(1)} %get-tuple-element.7), channel_id=1, source_target_pairs={{0,13},{1,12},{2,15},{3,14},{4,9},{5,8},{6,11},{7,10},{8,5},{9,4},... | collective-permute-start | bytes 49160 | tf_op jit(solution)/shard_map/ppermute | solution.py:29
  126.6 6.7 %collective-permute-start.13 = (bf16[128,64]{1,0:T(8,128)(2,1)S(1)}, bf16[128,64]{1,0:T(8,128)(2,1)S(1)}, u32[]{:S(2)}, u32[]{:S(2)}) collective-permute-start(bf16[128,64]{1,0:T(8,128)(2,1)S(1)} %get-tuple-element.6), channel_id=1, source_target_pairs={{0,14},{1,15},{2,12},{3,13},{4,10},{5,11},{6,8},{7,9},{8,6},{9,7},... | collective-permute-start | bytes 49160 | tf_op jit(solution)/shard_map/ppermute | solution.py:29
  128.6 6.4 %collective-permute-start.14 = (bf16[128,64]{1,0:T(8,128)(2,1)S(1)}, bf16[128,64]{1,0:T(8,128)(2,1)S(1)}, u32[]{:S(2)}, u32[]{:S(2)}) collective-permute-start(bf16[128,64]{1,0:T(8,128)(2,1)S(1)} %get-tuple-element.5), channel_id=1, source_target_pairs={{0,15},{1,14},{2,13},{3,12},{4,11},{5,10},{6,9},{7,8},{8,7},{9,6},... | collective-permute-start | bytes 49160 | tf_op jit(solution)/shard_map/ppermute | solution.py:29
Sparse Core Ops, SparseCore 0:
  9.5 44.1 all-gather.2
  55.9 49.0 all-gather.4
